TPU v7x, 32 devices: a whole 2x2x4 slice. The times are simulated.
32 devices in a mesh: dp: 8 (over z, y), row: 2 (over core), col: 2 (over x).
Axes of the slice: x: 2, y: 2, z: 4, core: 2. Of those that a mesh axis runs over, the one named last changes fastest.
Arguments:
- hidden_in: bfloat16 [4096, 960], P(('dp', 'col'), 'row')
- segment_ids: int32 [4096], P('dp'), may hold values from 0 to 4095, as said below
- position_ids: int32 [4096], P('dp'), may hold values from 0 to 2048, as said below
- attn_gain: float32 [960], P('row'), may hold values from 0.5 to 1.5
- query_weight: bfloat16 [960, 960], P('row', 'col')
- key_weight: bfloat16 [960, 320], P('row', 'col')
- value_matrix: bfloat16 [960, 320], P('row', 'col'), may hold values from -0.1875 to 0.1875
- output_weight: bfloat16 [960, 960], P('col', 'row'), may hold values from -0.75 to 0.75
- ffn_gain: float32 [960], P('row'), may hold values from 0.5 to 1.5
- gate_weight: bfloat16 [960, 2560], P('row', 'col'), may hold values from -0.1875 to 0.1875
- up_weight: bfloat16 [960, 2560], P('row', 'col'), may hold values from -0.1875 to 0.1875
- down_weight: bfloat16 [2560, 960], P('col', 'row'), may hold values from -0.125 to 0.125
- out_grad: bfloat16 [4096, 960], P(('dp', 'col'), 'row')
Outputs:
- hidden_out: bfloat16 [4096, 960], P(('dp', 'col'), 'row')
- hidden_in_grad: float32 [4096, 960], P(('dp', 'col'), 'row')
- attn_gain_grad: float32 [960], P('row')
- query_weight_grad: float32 [960, 960], P('row', 'col')
- key_weight_grad: float32 [960, 320], P('row', 'col')
- value_weight_grad: float32 [960, 320], P('row', 'col')
- output_weight_grad: float32 [960, 960], P('col', 'row')
- ffn_gain_grad: float32 [960], P('row')
- gate_weight_grad: float32 [2, 960, 1280], P('col', 'row', 'dp')
- up_weight_grad: float32 [2, 960, 1280], P('col', 'row', 'dp')
- down_weight_grad: float32 [2, 1280, 960], P('col', 'dp', 'row')
Inputs may be any that keep to these rules, and one draw needn't show every extreme that they name: `segment_ids`: segment numbers never fall from one token to the next, and the first token of each sequence of 512 tokens begins a new number. `position_ids`: within a document each token's position is one or two more than the previous token's; the first token of each sequence of 512 tokens has position 0.
All inputs are finite; a program needn't handle non-finite values.
Results may differ from a plain program's by a relative error of at most 0.02.
The roundings to bfloat16 on the way count: a program that leaves them out, or rounds other values in their place, can miss the bound.
Values may be sent and summed in bfloat16 or wider, within the bound.
A program may use at most 128 MiB of HBM per device.

v0:
```python
import jax
import jax.numpy as jnp
from jax import lax
from jax.sharding import PartitionSpec as P

MODEL_WIDTH = 960
QUERY_HEADS = 15
KEY_VALUE_HEADS = 5
HEAD_SIZE = 64
epsilon = 1e-05
rope_base = 10000.0
masked_score = -1e30


def rope_tables(position_row):
    half_size = HEAD_SIZE // 2
    frequency = rope_base ** (-(jnp.arange(half_size, dtype=jnp.float32) * 2.0) / HEAD_SIZE)
    angles = position_row.astype(jnp.float32)[:, None] * frequency[None, :]
    return (jnp.cos(angles), jnp.sin(angles))


def apply_rotary(values, cosine_table, sine_lookup, direction):
    half_size = values.shape[-1] // 2
    front_half = values[..., :half_size]
    back_half = values[..., half_size:]
    cosine_wide = cosine_table[:, None, :]
    sine_wide = direction * sine_lookup[:, None, :]
    return jnp.concatenate(
        [
            front_half * cosine_wide - back_half * sine_wide,
            back_half * cosine_wide + front_half * sine_wide,
        ],
        axis=-1,
    )


def matmul(left, right):
    return jnp.dot(left, right, preferred_element_type=jnp.float32)


def contract_rows(left, right):
    return lax.dot_general(
        left, right, (((0,), (0,)), ((), ())), preferred_element_type=jnp.float32
    )


def row_sums(values):
    return lax.psum(values, "row")


def gather_over_cols(values):
    return lax.all_gather(values, "col", axis=0, tiled=True)


def gather_over_rows(values):
    return lax.all_gather(values, "row", axis=0, tiled=True)


def sum_over_rows(partial_value):
    return lax.psum_scatter(partial_value, "row", scatter_dimension=0, tiled=True)


def sum_over_cols(partial_value):
    return lax.psum_scatter(partial_value, "col", scatter_dimension=0, tiled=True)


def to_heads(values):
    return lax.all_to_all(values, "col", split_axis=0, concat_axis=1, tiled=True)


def from_heads(values):
    return lax.all_to_all(values, "col", split_axis=1, concat_axis=0, tiled=True)


def norm_forward(residual, gain):
    mean_square = row_sums(jnp.sum(residual * residual, axis=1)) / MODEL_WIDTH
    inverse_rms = lax.rsqrt(mean_square + epsilon)
    unit_rows = residual * inverse_rms[:, None]
    return (unit_rows, inverse_rms, (unit_rows * gain[None, :]).astype(jnp.bfloat16))


def norm_backward(grad_normed, unit_rows, inverse_rms, gain):
    weighted = grad_normed * gain[None, :]
    inner_mean = row_sums(jnp.sum(weighted * unit_rows, axis=1)) / MODEL_WIDTH
    grad_input = inverse_rms[:, None] * (weighted - unit_rows * inner_mean[:, None])
    return (grad_input, jnp.sum(grad_normed * unit_rows, axis=0))


def attention_scores(query_group, key_group, allowed):
    scores = jnp.einsum(
        "qkgd,skd->kgqs", query_group, key_group, preferred_element_type=jnp.float32
    ) * HEAD_SIZE ** (-0.5)
    return jnp.where(allowed[None, None], scores, masked_score)


def on_device(
    hidden_in,
    segment_ids,
    position_ids,
    attn_gain,
    query_weight,
    key_weight,
    value_matrix,
    output_weight,
    ffn_gain,
    gate_weight,
    up_weight,
    down_weight,
    out_grad,
):
    n_rows = lax.axis_size("row")
    n_cols = lax.axis_size("col")
    sequence_length = segment_ids.shape[0]
    portion_length = sequence_length // (n_rows * n_cols)
    part_start = (lax.axis_index("row") * n_cols + lax.axis_index("col")) * portion_length
    query_cols = query_weight.shape[1]
    kv_cols = key_weight.shape[1]
    block_cols = query_cols + 2 * kv_cols
    heads_per_group = QUERY_HEADS // KEY_VALUE_HEADS
    ffn_cols = gate_weight.shape[1]
    residual = hidden_in.astype(jnp.float32)
    unit_one, inverse_one, normed_one = norm_forward(residual, attn_gain)
    normed_one_all = gather_over_cols(normed_one)
    proj_weight = jnp.concatenate([query_weight, key_weight, value_matrix], axis=1)
    projected = sum_over_rows(matmul(normed_one_all, proj_weight)).astype(jnp.bfloat16)
    grouped = to_heads(projected).reshape(portion_length, n_cols, block_cols)
    query_part = grouped[:, :, :query_cols].reshape(portion_length, n_cols * query_cols)
    key_portion = grouped[:, :, query_cols : query_cols + kv_cols].reshape(
        portion_length, n_cols * kv_cols
    )
    value_part = grouped[:, :, query_cols + kv_cols :].reshape(portion_length, n_cols * kv_cols)
    cosine_table, sine_lookup = rope_tables(
        lax.dynamic_slice_in_dim(position_ids, part_start, portion_length)
    )
    query_rotated = apply_rotary(
        query_part.astype(jnp.float32).reshape(portion_length, QUERY_HEADS, HEAD_SIZE),
        cosine_table,
        sine_lookup,
        1.0,
    ).astype(jnp.bfloat16)
    key_rotated = apply_rotary(
        key_portion.astype(jnp.float32).reshape(portion_length, KEY_VALUE_HEADS, HEAD_SIZE),
        cosine_table,
        sine_lookup,
        1.0,
    ).astype(jnp.bfloat16)
    key_token_rows, value_token_rows = (
        lax.all_gather(
            key_rotated.reshape(portion_length, KEY_VALUE_HEADS * HEAD_SIZE),
            ("row", "col"),
            axis=0,
            tiled=True,
        ),
        lax.all_gather(value_part, ("row", "col"), axis=0, tiled=True),
    )
    part_segments = lax.dynamic_slice_in_dim(segment_ids, part_start, portion_length)
    query_index = part_start + jnp.arange(portion_length, dtype=jnp.int32)
    key_index = jnp.arange(sequence_length, dtype=jnp.int32)
    allowed = (part_segments[:, None] == segment_ids[None, :]) & (
        key_index[None, :] <= query_index[:, None]
    )
    query_group = query_rotated.reshape(portion_length, KEY_VALUE_HEADS, heads_per_group, HEAD_SIZE)
    key_group = key_token_rows.reshape(sequence_length, KEY_VALUE_HEADS, HEAD_SIZE)
    value_group = value_token_rows.reshape(sequence_length, KEY_VALUE_HEADS, HEAD_SIZE)
    scores = attention_scores(query_group, key_group, allowed)
    row_max = jnp.max(scores, axis=-1, keepdims=True)
    log_total = row_max + jnp.log(jnp.sum(jnp.exp(scores - row_max), axis=-1, keepdims=True))
    attn_probs = jnp.exp(scores - log_total).astype(jnp.bfloat16)
    attended_output = (
        jnp.einsum("kgqs,skd->qkgd", attn_probs, value_group, preferred_element_type=jnp.float32)
        .astype(jnp.bfloat16)
        .reshape(portion_length, QUERY_HEADS * HEAD_SIZE)
    )
    attended_rows = from_heads(attended_output)
    attended_all = gather_over_rows(attended_rows)
    mid = residual + sum_over_cols(matmul(attended_all, output_weight))
    unit_two, inverse_two, normed_two = norm_forward(mid, ffn_gain)
    normed_two_all = gather_over_cols(normed_two)
    ffn_weight = jnp.concatenate([gate_weight, up_weight], axis=1)
    ffn_pre = sum_over_rows(matmul(normed_two_all, ffn_weight))
    gate_pre = ffn_pre[:, :ffn_cols]
    up_pre = ffn_pre[:, ffn_cols:]
    gate_sigmoid = jax.nn.sigmoid(gate_pre)
    gate_silu = gate_pre * gate_sigmoid
    inner_act = (gate_silu * up_pre).astype(jnp.bfloat16)
    inner_all = gather_over_rows(inner_act)
    final = mid + sum_over_cols(matmul(inner_all, down_weight))
    hidden_out = final.astype(jnp.bfloat16)
    grad_all = gather_over_cols(out_grad)
    inner_back = gather_over_rows(inner_act)
    down_wgrad = contract_rows(inner_back, grad_all)
    inner_grad = sum_over_rows(matmul(grad_all, down_weight.T))
    silu_slope = gate_sigmoid * (1.0 + gate_pre * (1.0 - gate_sigmoid))
    both_grad = jnp.concatenate(
        [
            (inner_grad * up_pre * silu_slope).astype(jnp.bfloat16),
            (inner_grad * gate_silu).astype(jnp.bfloat16),
        ],
        axis=1,
    )
    both_all = gather_over_rows(both_grad)
    normed_two_back = gather_over_cols(normed_two)
    ffn_wgrad = contract_rows(normed_two_back, both_all)
    normed_two_grad = sum_over_cols(matmul(both_all, ffn_weight.T))
    mid_part, ffn_gain_part = norm_backward(normed_two_grad, unit_two, inverse_two, ffn_gain)
    mid_grad = out_grad.astype(jnp.float32) + mid_part
    mid_grad_all = gather_over_cols(mid_grad.astype(jnp.bfloat16))
    attended_back = gather_over_rows(attended_rows)
    out_wgrad = contract_rows(attended_back, mid_grad_all)
    attended_gradient = to_heads(
        sum_over_rows(matmul(mid_grad_all, output_weight.T)).astype(jnp.bfloat16)
    )
    gradient_group = attended_gradient.reshape(
        portion_length, KEY_VALUE_HEADS, heads_per_group, HEAD_SIZE
    )
    attended_group = attended_output.reshape(
        portion_length, KEY_VALUE_HEADS, heads_per_group, HEAD_SIZE
    )
    grad_dot = jnp.transpose(
        jnp.sum(gradient_group.astype(jnp.float32) * attended_group.astype(jnp.float32), axis=-1),
        (1, 2, 0),
    )
    scores_again = attention_scores(query_group, key_group, allowed)
    prob_exact = jnp.exp(scores_again - log_total)
    value_gradient = jnp.einsum(
        "kgqs,qkgd->skd",
        prob_exact.astype(jnp.bfloat16),
        gradient_group,
        preferred_element_type=jnp.float32,
    )
    prob_grad = jnp.einsum(
        "qkgd,skd->kgqs", gradient_group, value_group, preferred_element_type=jnp.float32
    )
    score_grad = (prob_exact * (prob_grad - grad_dot[..., None]) * HEAD_SIZE ** (-0.5)).astype(
        jnp.bfloat16
    )
    query_grad = jnp.einsum(
        "kgqs,skd->qkgd", score_grad, key_group, preferred_element_type=jnp.float32
    )
    key_gradient = jnp.einsum(
        "kgqs,qkgd->skd", score_grad, query_group, preferred_element_type=jnp.float32
    )
    key_gradient_total, value_total = (
        lax.psum_scatter(
            key_gradient.reshape(sequence_length, KEY_VALUE_HEADS * HEAD_SIZE),
            ("row", "col"),
            scatter_dimension=0,
            tiled=True,
        ),
        lax.psum_scatter(
            value_gradient.reshape(sequence_length, KEY_VALUE_HEADS * HEAD_SIZE),
            ("row", "col"),
            scatter_dimension=0,
            tiled=True,
        ),
    )
    query_back = apply_rotary(
        query_grad.reshape(portion_length, QUERY_HEADS, HEAD_SIZE), cosine_table, sine_lookup, -1.0
    ).astype(jnp.bfloat16)
    key_backward = apply_rotary(
        key_gradient_total.reshape(portion_length, KEY_VALUE_HEADS, HEAD_SIZE),
        cosine_table,
        sine_lookup,
        -1.0,
    ).astype(jnp.bfloat16)
    regrouped = jnp.concatenate(
        [
            query_back.reshape(portion_length, n_cols, query_cols),
            key_backward.reshape(portion_length, n_cols, kv_cols),
            value_total.astype(jnp.bfloat16).reshape(portion_length, n_cols, kv_cols),
        ],
        axis=2,
    ).reshape(portion_length, n_cols * block_cols)
    proj_grad = from_heads(regrouped)
    proj_all = gather_over_rows(proj_grad)
    normed_one_back = gather_over_cols(normed_one)
    proj_wgrad = contract_rows(normed_one_back, proj_all)
    normed_one_grad = sum_over_cols(matmul(proj_all, proj_weight.T))
    in_part, attn_gain_part = norm_backward(normed_one_grad, unit_one, inverse_one, attn_gain)
    hidden_in_grad = mid_grad + in_part
    query_wgrad = proj_wgrad[:, :query_cols]
    key_wgrad = proj_wgrad[:, query_cols : query_cols + kv_cols]
    value_wgrad = proj_wgrad[:, query_cols + kv_cols :]
    col_gains = lax.psum((attn_gain_part, ffn_gain_part), "col")
    joined = lax.psum(
        (query_wgrad, key_wgrad, value_wgrad, out_wgrad, col_gains[0], col_gains[1]), "dp"
    )
    attn_totals = (joined[0], joined[1], joined[2], joined[3])
    gain_totals = (joined[4], joined[5])
    mlp_totals = (
        lax.psum_scatter(ffn_wgrad[None, :, :ffn_cols], "dp", scatter_dimension=2, tiled=True),
        lax.psum_scatter(ffn_wgrad[None, :, ffn_cols:], "dp", scatter_dimension=2, tiled=True),
        lax.psum_scatter(down_wgrad[None], "dp", scatter_dimension=1, tiled=True),
    )
    return (
        hidden_out,
        hidden_in_grad,
        gain_totals[0],
        attn_totals[0],
        attn_totals[1],
        attn_totals[2],
        attn_totals[3],
        gain_totals[1],
        mlp_totals[0],
        mlp_totals[1],
        mlp_totals[2],
    )


def solution(mesh):
    return jax.shard_map(
        on_device,
        mesh=mesh,
        in_specs=(
            P(("dp", "col"), "row"),
            P("dp"),
            P("dp"),
            P("row"),
            P("row", "col"),
            P("row", "col"),
            P("row", "col"),
            P("col", "row"),
            P("row"),
            P("row", "col"),
            P("row", "col"),
            P("col", "row"),
            P(("dp", "col"), "row"),
        ),
        out_specs=(
            P(("dp", "col"), "row"),
            P(("dp", "col"), "row"),
            P("row"),
            P("row", "col"),
            P("row", "col"),
            P("row", "col"),
            P("col", "row"),
            P("row"),
            P("col", "row", "dp"),
            P("col", "row", "dp"),
            P("col", "dp", "row"),
        ),
        check_vma=False,
    )
```

profile of v0, /device:TPU:0, one launch (start us, length us, event | category | flops | bytes accessed | tf_op | source)
XLA Modules:
  0.0 676.4 jit_solution(15995002472358062000)
XLA Ops:
  8.4 2.6 psum.84
  12.1 9.8 %all_gather.34 = bf16[512,480]{0,1:T(8,128)(2,1)S(1)} all-gather(bf16[256,480]{0,1:T(8,128)(2,1)S(1)} %fusion.10), channel_id=1, replica_groups=mesh['dp'=8,'row'=2,'col'=2] {'col'}, dimensions={0}, use_global_device_ids=true | all-gather | bytes 737280 | tf_op jit(solution)/shard_map/all_gather | solution.py:52
  21.8 1.2 copy.67
  23.1 1.1 copy.66
  24.2 3.2 fusion.18
  28.5 9.7 %reduce-scatter.11.cloned.1.call-done = f32[256,800]{0,1:T(8,128)} async-done(((f32[512,800]{0,1:T(8,128)}), f32[256,800]{0,1:T(8,128)}) %reduce-scatter.11.cloned.1.call-update) | async-done | bytes 819216 | tf_op jit(solution)/shard_map/reduce_scatter | solution.py:60
  38.2 1.9 copy_bitcast_fusion.1
  40.2 3.5 all-to-all-start
  43.8 7.3 %all-to-all-done = bf16[2,128,800]{1,2,0:T(8,128)(2,1)S(1)} async-done(((bf16[2,128,800]{1,2,0:T(8,128)(2,1)}), bf16[2,128,800]{1,2,0:T(8,128)(2,1)S(1)}, u32[]{:S(2)}, u32[]{:S(2)}) %all-to-all-start) | async-done | bytes 409632 | tf_op jit(solution)/shard_map/all_to_all | solution.py:68
  51.2 10.6 %all_gather.35 = bf16[512,320]{0,1:T(8,128)(2,1)S(1)} all-gather(bf16[128,320]{0,1:T(8,128)(2,1)S(1)} %bitcast.147), channel_id=1, replica_groups=mesh['dp'=8,'row'=2,'col'=2] {'row','col'}, dimensions={0}, use_global_device_ids=true | all-gather | bytes 409600 | tf_op jit(solution)/shard_map/all_gather | solution.py:154
  61.8 10.6 %all_gather.36 = bf16[512,320]{0,1:T(8,128)(2,1)S(1)} all-gather(bf16[128,320]{0,1:T(8,128)(2,1)S(1)} %bitcast.148), channel_id=1, replica_groups=mesh['dp'=8,'row'=2,'col'=2] {'row','col'}, dimensions={0}, use_global_device_ids=true | all-gather | bytes 409600 | tf_op jit(solution)/shard_map/all_gather | solution.py:148
  75.3 8.1 %all_to_all.67 = bf16[128,2,480]{0,2,1:T(8,128)(2,1)S(1)} all-to-all(bf16[128,2,480]{0,2,1:T(8,128)(2,1)S(1)} %bitcast.135), channel_id=1, replica_groups=mesh['dp'=8,'row'=2,'col'=2] {'col'}, dimensions={1} | all-to-all | bytes 491520 | tf_op jit(solution)/shard_map/all_to_all | solution.py:72
  83.4 2.2 all_gather.37
  85.6 1.4 fusion.36
  87.1 9.4 %all_gather.40 = bf16[512,480]{0,1:T(8,128)(2,1)S(1)} all-gather(bf16[256,480]{0,1:T(8,128)(2,1)S(1)} %copy-done.9), channel_id=1, replica_groups=mesh['dp'=8,'row'=2,'col'=2] {'col'}, dimensions={0}, use_global_device_ids=true | all-gather | bytes 737280 | tf_op jit(solution)/shard_map/all_gather | solution.py:52
  96.5 2.3 fusion.39
  98.9 2.5 constant_dynamic-update-slice_fusion.1
  101.4 2.5 constant_dynamic-update-slice_fusion
  103.9 3.6 reduce-scatter.13.cloned.1.call-done
  108.6 2.5 psum.85
  111.2 8.7 %all_gather.38 = bf16[512,480]{0,1:T(8,128)(2,1)S(1)} all-gather(bf16[256,480]{0,1:T(8,128)(2,1)S(1)} %multiply_convert_fusion.3), channel_id=1, replica_groups=mesh['dp'=8,'row'=2,'col'=2] {'col'}, dimensions={0}, use_global_device_ids=true | all-gather | bytes 737280 | tf_op jit(solution)/shard_map/all_gather | solution.py:52
  119.9 5.6 fusion.37
  125.6 13.3 %reduce-scatter.15.cloned.1.call-done = f32[256,2560]{1,0:T(8,128)} async-done(((f32[512,2560]{1,0:T(8,128)}), f32[256,2560]{1,0:T(8,128)}) %reduce-scatter.15.cloned.1.call-update) | async-done | bytes 2621456 | tf_op jit(solution)/shard_map/reduce_scatter | solution.py:60
  138.9 3.7 multiply_convert_fusion.1
  142.6 1.2 pad_maximum_fusion
  143.9 12.8 %all-gather.5.cloned.1.call-done = bf16[512,2560]{1,0:T(8,128)(2,1)} async-done(((bf16[256,2560]{1,0:T(8,128)(2,1)}), bf16[512,2560]{1,0:T(8,128)(2,1)}) %all-gather.5.cloned.1.call-update) | async-done | bytes 2621456 | tf_op jit(solution)/shard_map/all_gather | solution.py:56
  156.6 4.9 fusion.40
  161.6 21.0 %reduce-scatter.21.cloned.1.call-done = f32[256,480]{0,1:T(8,128)} async-done(((f32[512,480]{0,1:T(8,128)}), f32[256,480]{0,1:T(8,128)}) %reduce-scatter.21.cloned.1.call-update) | async-done | bytes 491536 | tf_op jit(solution)/shard_map/reduce_scatter | solution.py:64
  182.6 1.9 multiply_reduce_fusion
  184.4 2.4 psum.86
  186.9 1.2 fusion.33
  188.1 8.7 %all_gather.42 = bf16[512,480]{0,1:T(8,128)(2,1)S(1)} all-gather(bf16[256,480]{0,1:T(8,128)(2,1)S(1)} %fusion.33), channel_id=1, replica_groups=mesh['dp'=8,'row'=2,'col'=2] {'col'}, dimensions={0}, use_global_device_ids=true | all-gather | bytes 737280 | tf_op jit(solution)/shard_map/all_gather | solution.py:52
  196.8 1.4 fusion.45
  198.2 8.4 %reduce-scatter.23.cloned.1.call-done = f32[256,480]{0,1:T(8,128)} async-done(((f32[512,480]{0,1:T(8,128)}), f32[256,480]{0,1:T(8,128)}) %reduce-scatter.23.cloned.1.call-update) | async-done | bytes 491536 | tf_op jit(solution)/shard_map/reduce_scatter | solution.py:60
  207.7 8.3 %all_to_all.68 = bf16[2,128,480]{1,2,0:T(8,128)(2,1)S(1)} all-to-all(bf16[2,128,480]{1,2,0:T(8,128)(2,1)S(1)} %copy_bitcast_fusion.3), channel_id=1, replica_groups=mesh['dp'=8,'row'=2,'col'=2] {'col'}, dimensions={0} | all-to-all | bytes 491520 | tf_op jit(solution)/shard_map/all_to_all | solution.py:68
  216.0 4.1 fusion.22
  220.2 1.2 multiply_reduce_fusion.1
  221.3 3.8 fusion.2
  225.2 1.3 copy-done.2
  226.4 1.6 fusion.20
  228.7 2.1 fusion.41
  231.6 11.2 %reduce-scatter.27.cloned.1.call-done = f32[128,320]{0,1:T(8,128)} async-done(((f32[512,320]{0,1:T(8,128)}), f32[128,320]{0,1:T(8,128)}) %reduce-scatter.27.cloned.1.call-update) | async-done | bytes 163856 | tf_op jit(solution)/shard_map/reduce_scatter | solution.py:250
  242.8 1.6 convert_element_type.114
  244.3 23.4 %reduce-scatter.25.cloned.1.call-done = f32[128,320]{0,1:T(8,128)} async-done(((f32[512,320]{0,1:T(8,128)}), f32[128,320]{0,1:T(8,128)}) %reduce-scatter.25.cloned.1.call-update) | async-done | bytes 163856 | tf_op jit(solution)/shard_map/reduce_scatter | solution.py:244
  269.9 9.2 %all_to_all.69 = bf16[128,2,800]{0,2,1:T(8,128)(2,1)S(1)} all-to-all(bf16[128,2,800]{0,2,1:T(8,128)(2,1)S(1)} %pad_maximum_fusion.2), channel_id=1, replica_groups=mesh['dp'=8,'row'=2,'col'=2] {'col'}, dimensions={1} | all-to-all | bytes 819200 | tf_op jit(solution)/shard_map/all_to_all | solution.py:72
  279.1 2.4 all_gather.43
  282.4 1.6 fusion.17
  284.1 3.7 convolution_bitcast_fusion
  287.8 6.5 copy.78
  294.3 3.1 fusion.38
  297.5 3.2 fusion.44
  300.7 2.5 slice_bitcast_fusion
  303.2 6.4 copy.76
  309.7 6.5 copy.77
  316.2 1.4 fusion.43
  322.1 1.3 fusion.15
  323.4 4.9 all-reduce.5
  328.3 22.6 %all-reduce.3 = (f32[480]{0:T(512)}, f32[480]{0:T(512)}) all-reduce(f32[480]{0:T(512)S(1)} %get-tuple-element.68, f32[480]{0:T(512)S(1)} %get-tuple-element.69), channel_id=1, replica_groups=mesh['dp'=8,'row'=2,'col'=2] {'dp'}, use_global_device_ids=true, to_apply=%region_23.24 | all-reduce | flops 960 | bytes 7680 | tf_op jit(solution)/shard_map/psum | solution.py:285
  350.9 2.4 psum.87
  353.4 2.3 fusion.14
  355.7 304.2 %all-reduce.8.cloned.1.call-done = (f32[480,480]{0,1:T(8,128)}, f32[480,160]{0,1:T(8,128)}, f32[480,160]{0,1:T(8,128)}, f32[480,480]{1,0:T(8,128)}, f32[1,480,12...) async-done(((f32[480,480]{0,1:T(8,128)}, f32[480,160]{0,1:T(8,128)}, f32[480,160]{0,1:T(8,128)}, f32[480,480]{1,0:T(8,128)}, ...) | async-done | bytes 9830416 | tf_op jit(solution)/shard_map/psum | solution.py:285
  659.9 2.5 copy.79
  662.4 1.6 constant_dynamic-slice_fusion.1
  665.5 1.2 constant_dynamic-slice_fusion
  (144 shorter events, 22.2 us)
Async XLA Ops:
  7.2 89.3 %copy-start = (bf16[1280,480]{0,1:T(8,128)(2,1)S(1)}, bf16[1280,480]{0,1:T(8,128)(2,1)}, u32[]{:S(2)}) copy-start(bf16[1280,480]{0,1:T(8,128)(2,1)} %param.24) | copy-start | bytes 3686404
  7.2 31.0 %reduce-scatter.11.cloned.1.call-start = ((), (), s32[]{:S(2)}) async-start(), calls=%async_computation.14 | async-start | bytes 2457600 | tf_op jit(solution)/shard_map/reduce_scatter | solution.py:60
  21.8 5.7 copy-start.11
  23.1 4.4 copy-start.25
  24.2 3.3 copy-start.27
  24.2 3.3 copy-start.33
  40.2 11.0 %all-to-all-start = ((bf16[2,128,800]{1,2,0:T(8,128)(2,1)}), bf16[2,128,800]{1,2,0:T(8,128)(2,1)S(1)}, u32[]{:S(2)}, u32[]{:S(2)}) async-start(bf16[2,128,800]{1,2,0:T(8,128)(2,1)} %copy_bitcast_fusion.1), calls=%async_computation.1 | async-start | bytes 819200 | tf_op jit(solution)/shard_map/all_to_all | solution.py:68
  43.6 63.8 %reduce-scatter.13.cloned.1.call-start = ((), (), s32[]{:S(2)}) async-start(), calls=%async_computation.15 | async-start | bytes 1474560 | tf_op jit(solution)/shard_map/reduce_scatter | solution.py:64
  61.8 12.4 %copy-start.22 = (bf16[512,320]{0,1:T(8,128)(2,1)}, bf16[512,320]{0,1:T(8,128)(2,1)S(1)}, u32[]{:S(2)}) copy-start(bf16[512,320]{0,1:T(8,128)(2,1)S(1)} %all_gather.35) | copy-start | bytes 983044
  72.4 0.9 copy-start.8
  72.5 0.8 copy-start.17
  72.6 1.6 copy-start.15
  73.3 1.9 copy-start.1
  74.2 1.1 copy-start.31
  74.2 11.4 %copy-start.13 = (bf16[480,480]{1,0:T(8,128)(2,1)S(1)}, bf16[480,480]{1,0:T(8,128)(2,1)}, u32[]{:S(2)}) copy-start(bf16[480,480]{1,0:T(8,128)(2,1)} %param.20) | copy-start | bytes 1382404
  75.3 8.1 %copy-start.20 = (bf16[5,64,3,128]{3,1,2,0:T(8,128)(2,1)}, bf16[5,64,3,128]{3,1,2,0:T(8,128)(2,1)S(1)}, u32[]{:S(2)}) copy-start(bf16[5,64,3,128]{3,1,2,0:T(8,128)(2,1)S(1)} %convolution_convert_fusion) | copy-start | bytes 737284
  75.3 11.7 %copy-start.9 = (bf16[256,480]{0,1:T(8,128)(2,1)S(1)}, bf16[256,480]{0,1:T(8,128)(2,1)}, u32[]{:S(2)}) copy-start(bf16[256,480]{0,1:T(8,128)(2,1)} %param.25) | copy-start | bytes 737284
  87.0 38.6 %reduce-scatter.19.cloned.1.call-start = ((), (), s32[]{:S(2)}) async-start(), calls=%async_computation.19 | async-start | bytes 3932160 | tf_op jit(solution)/shard_map/reduce_scatter | solution.py:60
  96.5 2.3 copy-start.7
  98.9 8.6 %copy-start.3 = (bf16[256,480]{0,1:T(8,128)(2,1)S(1)}, bf16[256,480]{0,1:T(8,128)(2,1)}, u32[]{:S(2)}) copy-start(bf16[256,480]{0,1:T(8,128)(2,1)} %param.13) | copy-start | bytes 737284
  98.9 40.1 %reduce-scatter.15.cloned.1.call-start = ((), (), s32[]{:S(2)}) async-start(), calls=%async_computation.16 | async-start | bytes 7864320 | tf_op jit(solution)/shard_map/reduce_scatter | solution.py:60
  101.4 9.6 %copy-start.29 = (f32[480]{0:T(512)S(1)}, f32[480]{0:T(512)}, u32[]{:S(2)}) copy-start(f32[480]{0:T(512)} %param.21) | copy-start | bytes 5764
  125.5 31.1 %all-gather.5.cloned.1.call-start = ((), (), s32[]{:S(2)}) async-start(), calls=%async_computation.20 | async-start | bytes 3932160 | tf_op jit(solution)/shard_map/all_gather | solution.py:56
  143.8 38.7 %reduce-scatter.21.cloned.1.call-start = ((), (), s32[]{:S(2)}) async-start(), calls=%async_computation.21 | async-start | bytes 1474560 | tf_op jit(solution)/shard_map/reduce_scatter | solution.py:64
  161.5 45.1 %reduce-scatter.23.cloned.1.call-start = ((), (), s32[]{:S(2)}) async-start(), calls=%async_computation.22 | async-start | bytes 1474560 | tf_op jit(solution)/shard_map/reduce_scatter | solution.py:60
  186.8 10.0 %copy-start.14 = (bf16[480,480]{1,0:T(8,128)(2,1)S(1)}, bf16[480,480]{1,0:T(8,128)(2,1)}, u32[]{:S(2)}) copy-start(bf16[480,480]{1,0:T(8,128)(2,1)} %param.20) | copy-start | bytes 1382404
  198.2 44.6 %reduce-scatter.27.cloned.1.call-start = ((), (), s32[]{:S(2)}) async-start(), calls=%async_computation.24 | async-start | bytes 819200 | tf_op jit(solution)/shard_map/reduce_scatter | solution.py:250
  216.0 4.1 copy-start.21
  220.1 47.7 %reduce-scatter.25.cloned.1.call-start = ((), (), s32[]{:S(2)}) async-start(), calls=%async_computation.23 | async-start | bytes 819200 | tf_op jit(solution)/shard_map/reduce_scatter | solution.py:244
  221.3 5.1 copy-start.16
  221.3 5.1 copy-start.18
  225.1 1.3 copy-start.2
  228.1 56.1 %all-gather.3.cloned.1.call-start = ((), (), s32[]{:S(2)}) async-start(), calls=%async_computation.17 | async-start | bytes 1966080 | tf_op jit(solution)/shard_map/all_gather | solution.py:56
  228.6 93.4 %reduce-scatter.29.cloned.1.call-start = ((), (), s32[]{:S(2)}) async-start(), calls=%async_computation.25 | async-start | bytes 1474560 | tf_op jit(solution)/shard_map/reduce_scatter | solution.py:64
  267.8 14.6 %copy-start.26 = (bf16[480,160]{1,0:T(8,128)(2,1)S(1)}, bf16[480,160]{1,0:T(8,128)(2,1)}, u32[]{:S(2)}) copy-start(bf16[480,160]{1,0:T(8,128)(2,1)} %copy-done.25) | copy-start | bytes 460804
  267.8 14.6 %copy-start.28 = (bf16[480,160]{1,0:T(8,128)(2,1)S(1)}, bf16[480,160]{1,0:T(8,128)(2,1)}, u32[]{:S(2)}) copy-start(bf16[480,160]{1,0:T(8,128)(2,1)} %copy-done.27) | copy-start | bytes 460804
  267.8 14.6 %copy-start.34 = (bf16[480,480]{1,0:T(8,128)(2,1)S(1)}, bf16[480,480]{1,0:T(8,128)(2,1)}, u32[]{:S(2)}) copy-start(bf16[480,480]{1,0:T(8,128)(2,1)} %param.17) | copy-start | bytes 1382404
  281.5 0.9 copy-start.5
  284.1 69.3 %reduce-scatter.17.cloned.1.call-start = ((), (), s32[]{:S(2)}) async-start(), calls=%async_computation.18 | async-start | bytes 1474560 | tf_op jit(solution)/shard_map/reduce_scatter | solution.py:64
  297.4 362.4 %all-reduce.8.cloned.1.call-start = ((), (), s32[]{:S(2)}) async-start(), calls=%async_computation.26 | async-start | bytes 20971520 | tf_op jit(solution)/shard_map/psum | solution.py:285
  309.7 7.9 %copy-start.12 = (bf16[512,480]{0,1:T(8,128)(2,1)S(1)}, bf16[512,480]{0,1:T(8,128)(2,1)}, u32[]{:S(2)}) copy-start(bf16[512,480]{0,1:T(8,128)(2,1)} %copy-done.11) | copy-start | bytes 1474564
  316.2 1.4 copy-start.6
  320.2 0.7 copy-start.35
  320.2 1.9 copy-start.30
  320.2 3.2 copy-start.32
  320.2 33.2 %copy-start.4 = (f32[256,480]{0,1:T(8,128)S(1)}, f32[256,480]{0,1:T(8,128)}, u32[]{:S(2)}) copy-start(f32[256,480]{0,1:T(8,128)} %reduce-scatter.21.cloned.1.call-done) | copy-start | bytes 1474564
  320.2 33.2 %copy-start.10 = (bf16[256,480]{0,1:T(8,128)(2,1)S(1)}, bf16[256,480]{0,1:T(8,128)(2,1)}, u32[]{:S(2)}) copy-start(bf16[256,480]{0,1:T(8,128)(2,1)} %param.25) | copy-start | bytes 737284
  662.3 5.1 copy-start.24
  662.4 5.8 copy-start.23
  662.4 6.5 copy-start.19
Sparse Core Ops, SparseCore 0:
  27.6 10.5 reduce-scatter.10
  87.1 20.2 reduce-scatter.12
  109.7 10.6 reduce-scatter.18
  125.6 13.2 reduce-scatter.14
  143.9 12.6 all-gather.4
  161.7 20.8 reduce-scatter.20
  198.3 8.3 reduce-scatter.22
  220.2 22.5 reduce-scatter.26
  245.3 22.4 reduce-scatter.24
  269.7 9.4 all-gather.2
  284.2 19.6 reduce-scatter.28
  306.6 19.6 reduce-scatter.16
  332.3 327.4 all-reduce.7
where the time goes:
time: 678 us; the launch traced here: 676 us
  waiting for transfers between devices  416 us (61%)
  blocking collectives  125 us (18%)
  matrix products  45.8 us (7%)
  local copies, waits for them, and re-layouts  44.9 us (7%)
  other arithmetic  25.6 us (4%)
  between operations  15.1 us (2%)
    psum x1, waiting for transfers between devices, on_device(): lax.psum((query_wgrad, key_wgrad, value_wgrad, out_wgrad, col_gains[0], c...  304 us
    all_gather x4, blocking collectives, gather_over_cols(): return lax.all_gather(values, 'col', axis=0, tiled=True)  36.6 us
    reduce_scatter x4, waiting for transfers between devices, sum_over_rows(): lax.psum_scatter(partial_value, 'row', scatter_dimension=0, tiled=True)  31.5 us
    reduce_scatter x4, waiting for transfers between devices, sum_over_cols(): lax.psum_scatter(partial_value, 'col', scatter_dimension=0, tiled=True)  24.5 us
    dot_general x8, matrix products, matmul(): return jnp.dot(left, right, preferred_element_type=jnp.float32)  23.5 us
    reduce_scatter x1, waiting for transfers between devices, on_device(): lax.psum_scatter(key_gradient.reshape(sequence_length, KEY_VALUE_HEADS *...  23.4 us
    psum x1, blocking collectives, on_device(): lax.psum((query_wgrad, key_wgrad, value_wgrad, out_wgrad, col_gains[0], c...  22.6 us
    unnamed x85, local copies, waits for them, and re-layouts  18.3 us
  transfers between devices with their start and end apart: 14, of which 10 were waited for; matrix products, arithmetic and copies ran while one was open for 10% of the time, Pallas kernels for 0%

commit v1 on v0

--- a/solution.py
+++ b/solution.py
@@ -10,6 +10,29 @@
 epsilon = 1e-05
 rope_base = 10000.0
 masked_score = -1e30
+
+
+def laid_out(pieces, dim):
+    lengths = list(pieces.shape[1:])
+    lengths[dim] *= pieces.shape[0]
+    return jnp.moveaxis(pieces, 0, dim).reshape(lengths)
+
+
+def doubled(value, axis):
+    devices, mine = (lax.axis_size(axis), lax.axis_index(axis))
+    blocks, bit = (value[None], 1)
+    while bit < devices:
+        received = lax.ppermute(blocks, axis, [(i, i ^ bit) for i in range(devices)])
+        low = mine & bit == 0
+        blocks = jnp.concatenate(
+            [jnp.where(low, blocks, received), jnp.where(low, received, blocks)]
+        )
+        bit *= 2
+    return blocks
+
+
+def gather_by_bits(x, axis, dim):
+    return laid_out(doubled(x, axis), dim)
 
 
 def rope_tables(position_row):
@@ -49,7 +72,7 @@
 
 
 def gather_over_cols(values):
-    return lax.all_gather(values, "col", axis=0, tiled=True)
+    return gather_by_bits(values, "col", 0)
 
 
 def gather_over_rows(values):

time: 678 us -> 688 us (1.015)
  waiting for transfers between devices: 416 us -> 457 us
  blocking collectives: 125 us -> 89 us
    all_gather x4 -> x0, blocking collectives: 36.6 us -> none  [gather_over_cols(): return lax.all_gather(values, 'col', axis=0, tiled=True)]
    ppermute x0 -> x4, waiting for transfers between devices: none -> 18.7 us  [doubled(): lax.ppermute(blocks, axis, [(i, i ^ bit) for i in range(devices)])]
    reduce_scatter x4, waiting for transfers between devices: 24.5 us -> 40.6 us  [sum_over_cols(): lax.psum_scatter(partial_value, 'col', scatter_dimension=0, tiled=True)]
    unnamed x85 -> x94, local copies, waits for them, and re-layouts: 18.3 us -> 22 us
  transfers between devices with their start and end apart: 14 -> 18, of which waited for: 10 -> 14; matrix products, arithmetic and copies ran while one was open for 10% -> 9% of each run, Pallas kernels for 0% -> 0%
where the time goes in v1:
time: 688 us; the launch traced here: 687 us
  waiting for transfers between devices  457 us (66%)
  blocking collectives  89 us (13%)
  local copies, waits for them, and re-layouts  46.3 us (7%)
  matrix products  43.4 us (6%)
  other arithmetic  28.1 us (4%)
  between operations  15.2 us (2%)
  starting transfers between devices  8.09 us (1%)
    psum x1, waiting for transfers between devices, on_device(): lax.psum((query_wgrad, key_wgrad, value_wgrad, out_wgrad, col_gains[0], c...  304 us
    reduce_scatter x4, waiting for transfers between devices, sum_over_cols(): lax.psum_scatter(partial_value, 'col', scatter_dimension=0, tiled=True)  40.6 us
    reduce_scatter x4, waiting for transfers between devices, sum_over_rows(): lax.psum_scatter(partial_value, 'row', scatter_dimension=0, tiled=True)  37.8 us
    reduce_scatter x1, waiting for transfers between devices, on_device(): lax.psum_scatter(key_gradient.reshape(sequence_length, KEY_VALUE_HEADS *...  23.4 us
    psum x1, blocking collectives, on_device(): lax.psum((query_wgrad, key_wgrad, value_wgrad, out_wgrad, col_gains[0], c...  22.7 us
    unnamed x94, local copies, waits for them, and re-layouts  22 us
    dot_general x8, matrix products, matmul(): return jnp.dot(left, right, preferred_element_type=jnp.float32)  21 us
    ppermute x4, waiting for transfers between devices, doubled(): lax.ppermute(blocks, axis, [(i, i ^ bit) for i in range(devices)])  18.7 us
  transfers between devices with their start and end apart: 18, of which 14 were waited for; matrix products, arithmetic and copies ran while one was open for 9% of the time, Pallas kernels for 0%

profile of v1, /device:TPU:0, one launch (start us, length us, event | category | flops | bytes accessed | tf_op | source)
XLA Modules:
  0.0 686.7 jit_solution(6607611796754963276)
XLA Ops:
  7.2 1.2 fusion.16
  8.4 2.6 psum.84
  12.1 2.9 collective-permute-start
  17.2 4.1 collective-permute-done
  22.6 2.1 fusion.18
  25.7 9.7 %reduce-scatter.11.cloned.1.call-done = f32[256,800]{0,1:T(8,128)} async-done(((f32[512,800]{0,1:T(8,128)}), f32[256,800]{0,1:T(8,128)}) %reduce-scatter.11.cloned.1.call-update) | async-done | bytes 819216 | tf_op jit(solution)/shard_map/reduce_scatter | solution.py:83
  35.4 1.9 copy_bitcast_fusion.1
  37.4 3.5 all-to-all-start
  41.1 7.3 %all-to-all-done = bf16[2,128,800]{1,2,0:T(8,128)(2,1)S(1)} async-done(((bf16[2,128,800]{1,2,0:T(8,128)(2,1)}), bf16[2,128,800]{1,2,0:T(8,128)(2,1)S(1)}, u32[]{:S(2)}, u32[]{:S(2)}) %all-to-all-start) | async-done | bytes 409632 | tf_op jit(solution)/shard_map/all_to_all | solution.py:91
  48.4 10.6 %all_gather.20 = bf16[512,320]{0,1:T(8,128)(2,1)S(1)} all-gather(bf16[128,320]{0,1:T(8,128)(2,1)S(1)} %bitcast.181), channel_id=1, replica_groups=mesh['dp'=8,'row'=2,'col'=2] {'row','col'}, dimensions={0}, use_global_device_ids=true | all-gather | bytes 409600 | tf_op jit(solution)/shard_map/all_gather | solution.py:177
  59.0 10.6 %all_gather.21 = bf16[512,320]{0,1:T(8,128)(2,1)S(1)} all-gather(bf16[128,320]{0,1:T(8,128)(2,1)S(1)} %bitcast.182), channel_id=1, replica_groups=mesh['dp'=8,'row'=2,'col'=2] {'row','col'}, dimensions={0}, use_global_device_ids=true | all-gather | bytes 409600 | tf_op jit(solution)/shard_map/all_gather | solution.py:171
  73.6 8.1 %all_to_all.67 = bf16[128,2,480]{0,2,1:T(8,128)(2,1)S(1)} all-to-all(bf16[128,2,480]{0,2,1:T(8,128)(2,1)S(1)} %bitcast.169), channel_id=1, replica_groups=mesh['dp'=8,'row'=2,'col'=2] {'col'}, dimensions={1} | all-to-all | bytes 491520 | tf_op jit(solution)/shard_map/all_to_all | solution.py:95
  81.7 2.2 all_gather.22
  83.8 1.4 fusion.37
  85.7 19.6 %reduce-scatter.13.cloned.1.call-done = f32[256,480]{0,1:T(8,128)} async-done(((f32[512,480]{0,1:T(8,128)}), f32[256,480]{0,1:T(8,128)}) %reduce-scatter.13.cloned.1.call-update) | async-done | bytes 491536 | tf_op jit(solution)/shard_map/reduce_scatter | solution.py:87
  106.4 2.5 psum.85
  110.2 7.0 %collective-permute-done.1 = bf16[1,256,480]{1,2,0:T(8,128)(2,1)S(1)} collective-permute-done((bf16[1,256,480]{1,2,0:T(8,128)(2,1)S(1)}, bf16[1,256,480]{1,2,0:T(8,128)(2,1)S(1)}, u32[]{:S(2)}, u32[]{:S(2)}) %collective-permute-start.1) | collective-permute-done | bytes 245792 | tf_op jit(solution)/shard_map/ppermute | solution.py:25
  119.1 2.3 fusion.40
  121.6 1.5 constant_dynamic-update-slice_fusion.1
  123.4 1.3 copy-done.4
  124.7 4.2 fusion.38
  129.0 3.2 reduce-scatter.19.cloned.1.call-done
  132.2 16.5 %reduce-scatter.15.cloned.1.call-done = f32[256,2560]{1,0:T(8,128)} async-done(((f32[512,2560]{1,0:T(8,128)}), f32[256,2560]{1,0:T(8,128)}) %reduce-scatter.15.cloned.1.call-update) | async-done | bytes 2621456 | tf_op jit(solution)/shard_map/reduce_scatter | solution.py:83
  148.7 3.7 multiply_convert_fusion.1
  152.4 1.2 pad_maximum_fusion
  153.6 12.7 %all-gather.5.cloned.1.call-done = bf16[512,2560]{1,0:T(8,128)(2,1)} async-done(((bf16[256,2560]{1,0:T(8,128)(2,1)}), bf16[512,2560]{1,0:T(8,128)(2,1)}) %all-gather.5.cloned.1.call-update) | async-done | bytes 2621456 | tf_op jit(solution)/shard_map/all_gather | solution.py:79
  166.4 4.9 fusion.41
  171.3 20.9 %reduce-scatter.21.cloned.1.call-done = f32[256,480]{0,1:T(8,128)} async-done(((f32[512,480]{0,1:T(8,128)}), f32[256,480]{0,1:T(8,128)}) %reduce-scatter.21.cloned.1.call-update) | async-done | bytes 491536 | tf_op jit(solution)/shard_map/reduce_scatter | solution.py:87
  192.3 1.9 multiply_reduce_fusion
  194.1 2.6 psum.86
  196.8 1.2 convert_bitcast_fusion.2
  198.4 7.7 %collective-permute-done.3 = bf16[1,256,480]{1,2,0:T(8,128)(2,1)S(1)} collective-permute-done((bf16[1,256,480]{1,2,0:T(8,128)(2,1)S(1)}, bf16[1,256,480]{1,2,0:T(8,128)(2,1)S(1)}, u32[]{:S(2)}, u32[]{:S(2)}) %collective-permute-start.3) | collective-permute-done | bytes 245792 | tf_op jit(solution)/shard_map/ppermute | solution.py:25
  206.3 1.4 fusion.46
  207.7 8.4 %reduce-scatter.23.cloned.1.call-done = f32[256,480]{0,1:T(8,128)} async-done(((f32[512,480]{0,1:T(8,128)}), f32[256,480]{0,1:T(8,128)}) %reduce-scatter.23.cloned.1.call-update) | async-done | bytes 491536 | tf_op jit(solution)/shard_map/reduce_scatter | solution.py:83
  217.2 8.2 %all_to_all.68 = bf16[2,128,480]{1,2,0:T(8,128)(2,1)S(1)} all-to-all(bf16[2,128,480]{1,2,0:T(8,128)(2,1)S(1)} %copy_bitcast_fusion.3), channel_id=1, replica_groups=mesh['dp'=8,'row'=2,'col'=2] {'col'}, dimensions={0} | all-to-all | bytes 491520 | tf_op jit(solution)/shard_map/all_to_all | solution.py:91
  225.5 4.1 fusion.24
  230.8 3.8 fusion.2
  234.6 1.3 copy-done.3
  235.9 1.6 fusion.22
  238.2 2.1 fusion.42
  241.1 11.2 %reduce-scatter.27.cloned.1.call-done = f32[128,320]{0,1:T(8,128)} async-done(((f32[512,320]{0,1:T(8,128)}), f32[128,320]{0,1:T(8,128)}) %reduce-scatter.27.cloned.1.call-update) | async-done | bytes 163856 | tf_op jit(solution)/shard_map/reduce_scatter | solution.py:273
  252.3 1.6 convert_element_type.114
  253.8 23.4 %reduce-scatter.25.cloned.1.call-done = f32[128,320]{0,1:T(8,128)} async-done(((f32[512,320]{0,1:T(8,128)}), f32[128,320]{0,1:T(8,128)}) %reduce-scatter.25.cloned.1.call-update) | async-done | bytes 163856 | tf_op jit(solution)/shard_map/reduce_scatter | solution.py:267
  279.4 9.2 %all_to_all.69 = bf16[128,2,800]{0,2,1:T(8,128)(2,1)S(1)} all-to-all(bf16[128,2,800]{0,2,1:T(8,128)(2,1)S(1)} %pad_maximum_fusion.2), channel_id=1, replica_groups=mesh['dp'=8,'row'=2,'col'=2] {'col'}, dimensions={1} | all-to-all | bytes 819200 | tf_op jit(solution)/shard_map/all_to_all | solution.py:95
  288.6 2.4 all_gather.25
  291.9 1.6 fusion.17
  293.6 3.7 convolution_bitcast_fusion
  297.3 6.5 copy.90
  303.8 3.1 fusion.39
  307.0 3.2 fusion.45
  310.2 2.5 slice_bitcast_fusion
  312.7 6.4 copy.88
  319.1 6.6 copy.89
  325.7 1.4 fusion.44
  331.6 1.3 fusion.15
  332.8 4.9 all-reduce.5
  337.8 22.7 %all-reduce.3 = (f32[480]{0:T(512)}, f32[480]{0:T(512)}) all-reduce(f32[480]{0:T(512)S(1)} %get-tuple-element.68, f32[480]{0:T(512)S(1)} %get-tuple-element.69), channel_id=1, replica_groups=mesh['dp'=8,'row'=2,'col'=2] {'dp'}, use_global_device_ids=true, to_apply=%region_23.24 | all-reduce | flops 960 | bytes 7680 | tf_op jit(solution)/shard_map/psum | solution.py:308
  360.4 2.4 psum.87
  362.9 2.3 fusion.14
  365.2 304.2 %all-reduce.8.cloned.1.call-done = (f32[480,480]{0,1:T(8,128)}, f32[480,160]{0,1:T(8,128)}, f32[480,160]{0,1:T(8,128)}, f32[480,480]{1,0:T(8,128)}, f32[1,480,12...) async-done(((f32[480,480]{0,1:T(8,128)}, f32[480,160]{0,1:T(8,128)}, f32[480,160]{0,1:T(8,128)}, f32[480,480]{1,0:T(8,128)}, ...) | async-done | bytes 9830416 | tf_op jit(solution)/shard_map/psum | solution.py:308
  669.4 2.5 copy.91
  671.9 1.3 constant_dynamic-slice_fusion.2
  673.9 1.2 constant_dynamic-slice_fusion.1
  675.9 1.2 constant_dynamic-slice_fusion
  (168 shorter events, 30.9 us)
Async XLA Ops:
  7.2 112.0 %copy-start = (bf16[1280,480]{0,1:T(8,128)(2,1)S(1)}, bf16[1280,480]{0,1:T(8,128)(2,1)}, u32[]{:S(2)}) copy-start(bf16[1280,480]{0,1:T(8,128)(2,1)} %param.24) | copy-start | bytes 3686404
  7.2 15.3 %copy-start.37 = (bf16[480,480]{1,0:T(8,128)(2,1)S(1)}, bf16[480,480]{1,0:T(8,128)(2,1)}, u32[]{:S(2)}) copy-start(bf16[480,480]{1,0:T(8,128)(2,1)} %param.17) | copy-start | bytes 1382404
  7.2 28.2 %reduce-scatter.11.cloned.1.call-start = ((), (), s32[]{:S(2)}) async-start(), calls=%async_computation.14 | async-start | bytes 2457600 | tf_op jit(solution)/shard_map/reduce_scatter | solution.py:83
  12.1 9.2 %collective-permute-start = (bf16[1,256,480]{1,2,0:T(8,128)(2,1)S(1)}, bf16[1,256,480]{1,2,0:T(8,128)(2,1)S(1)}, u32[]{:S(2)}, u32[]{:S(2)}) collective-permute-start(bf16[1,256,480]{1,2,0:T(8,128)(2,1)S(1)} %fusion.21), channel_id=1, source_target_pairs={{0,1},{1,0},{2,3},{3,2},{4,5},{5,4},{6,7},{7,6},{8,9},{9,8},{10,11... | collective-permute-start | bytes 737288 | tf_op jit(solution)/shard_map/ppermute | solution.py:25
  16.1 8.6 %copy-start.27 = (bf16[480,160]{1,0:T(8,128)(2,1)}, bf16[480,160]{1,0:T(8,128)(2,1)S(1)}, u32[]{:S(2)}) copy-start(bf16[480,160]{1,0:T(8,128)(2,1)S(1)} %copy.76) | copy-start | bytes 460804
  17.2 7.5 %copy-start.29 = (bf16[480,160]{1,0:T(8,128)(2,1)}, bf16[480,160]{1,0:T(8,128)(2,1)S(1)}, u32[]{:S(2)}) copy-start(bf16[480,160]{1,0:T(8,128)(2,1)S(1)} %copy.75) | copy-start | bytes 460804
  22.5 2.2 copy-start.12
  22.5 2.2 copy-start.36
  37.4 11.0 %all-to-all-start = ((bf16[2,128,800]{1,2,0:T(8,128)(2,1)}), bf16[2,128,800]{1,2,0:T(8,128)(2,1)S(1)}, u32[]{:S(2)}, u32[]{:S(2)}) async-start(bf16[2,128,800]{1,2,0:T(8,128)(2,1)} %copy_bitcast_fusion.1), calls=%async_computation.1 | async-start | bytes 819200 | tf_op jit(solution)/shard_map/all_to_all | solution.py:91
  40.9 64.4 %reduce-scatter.13.cloned.1.call-start = ((), (), s32[]{:S(2)}) async-start(), calls=%async_computation.15 | async-start | bytes 1474560 | tf_op jit(solution)/shard_map/reduce_scatter | solution.py:87
  59.0 12.5 %copy-start.24 = (bf16[512,320]{0,1:T(8,128)(2,1)}, bf16[512,320]{0,1:T(8,128)(2,1)S(1)}, u32[]{:S(2)}) copy-start(bf16[512,320]{0,1:T(8,128)(2,1)S(1)} %all_gather.20) | copy-start | bytes 983044
  69.6 0.9 copy-start.9
  69.7 1.6 copy-start.17
  69.8 1.6 copy-start.19
  70.5 3.0 copy-start.1
  71.4 1.1 copy-start.34
  72.5 11.3 %copy-start.14 = (bf16[480,480]{1,0:T(8,128)(2,1)S(1)}, bf16[480,480]{1,0:T(8,128)(2,1)}, u32[]{:S(2)}) copy-start(bf16[480,480]{1,0:T(8,128)(2,1)} %param.20) | copy-start | bytes 1382404
  73.5 8.1 %copy-start.22 = (bf16[5,64,3,128]{3,1,2,0:T(8,128)(2,1)}, bf16[5,64,3,128]{3,1,2,0:T(8,128)(2,1)S(1)}, u32[]{:S(2)}) copy-start(bf16[5,64,3,128]{3,1,2,0:T(8,128)(2,1)S(1)} %convolution_convert_fusion) | copy-start | bytes 737284
  73.6 11.8 %copy-start.10 = (bf16[256,480]{0,1:T(8,128)(2,1)S(1)}, bf16[256,480]{0,1:T(8,128)(2,1)}, u32[]{:S(2)}) copy-start(bf16[256,480]{0,1:T(8,128)(2,1)} %param.25) | copy-start | bytes 737284
  73.6 31.7 %copy-start.2 = (bf16[256,480]{0,1:T(8,128)(2,1)S(1)}, bf16[256,480]{0,1:T(8,128)(2,1)}, u32[]{:S(2)}) copy-start(bf16[256,480]{0,1:T(8,128)(2,1)} %param.13) | copy-start | bytes 737284
  81.7 27.3 %copy-start.32 = (f32[480]{0:T(512)S(1)}, f32[480]{0:T(512)}, u32[]{:S(2)}) copy-start(f32[480]{0:T(512)} %param.21) | copy-start | bytes 5764
  85.3 46.9 %reduce-scatter.19.cloned.1.call-start = ((), (), s32[]{:S(2)}) async-start(), calls=%async_computation.19 | async-start | bytes 3932160 | tf_op jit(solution)/shard_map/reduce_scatter | solution.py:83
  85.3 24.2 %collective-permute-start.2 = (bf16[1,256,480]{1,2,0:T(8,128)(2,1)S(1)}, bf16[1,256,480]{1,2,0:T(8,128)(2,1)S(1)}, u32[]{:S(2)}, u32[]{:S(2)}) collective-permute-start(bf16[1,256,480]{1,2,0:T(8,128)(2,1)S(1)} %bitcast.159), channel_id=1, source_target_pairs={{0,1},{1,0},{2,3},{3,2},{4,5},{5,4},{6,7},{7,6},{8,9},{9,8},{10,11... | collective-permute-start | bytes 737288 | tf_op jit(solution)/shard_map/ppermute | solution.py:25
  109.1 8.1 %collective-permute-start.1 = (bf16[1,256,480]{1,2,0:T(8,128)(2,1)S(1)}, bf16[1,256,480]{1,2,0:T(8,128)(2,1)S(1)}, u32[]{:S(2)}, u32[]{:S(2)}) collective-permute-start(bf16[1,256,480]{1,2,0:T(8,128)(2,1)S(1)} %fusion.20), channel_id=1, source_target_pairs={{0,1},{1,0},{2,3},{3,2},{4,5},{5,4},{6,7},{7,6},{8,9},{9,8},{10,11... | collective-permute-start | bytes 737288 | tf_op jit(solution)/shard_map/ppermute | solution.py:25
  109.5 0.7 copy-start.31
  118.3 0.8 copy-start.8
  121.5 27.2 %reduce-scatter.15.cloned.1.call-start = ((), (), s32[]{:S(2)}) async-start(), calls=%async_computation.16 | async-start | bytes 7864320 | tf_op jit(solution)/shard_map/reduce_scatter | solution.py:83
  121.6 1.7 copy-start.16
  123.3 1.4 copy-start.4
  129.0 37.4 %all-gather.5.cloned.1.call-start = ((), (), s32[]{:S(2)}) async-start(), calls=%async_computation.20 | async-start | bytes 3932160 | tf_op jit(solution)/shard_map/all_gather | solution.py:79
  153.6 38.7 %reduce-scatter.21.cloned.1.call-start = ((), (), s32[]{:S(2)}) async-start(), calls=%async_computation.21 | async-start | bytes 1474560 | tf_op jit(solution)/shard_map/reduce_scatter | solution.py:87
  171.3 44.9 %reduce-scatter.23.cloned.1.call-start = ((), (), s32[]{:S(2)}) async-start(), calls=%async_computation.22 | async-start | bytes 1474560 | tf_op jit(solution)/shard_map/reduce_scatter | solution.py:83
  196.7 9.5 %copy-start.15 = (bf16[480,480]{1,0:T(8,128)(2,1)S(1)}, bf16[480,480]{1,0:T(8,128)(2,1)}, u32[]{:S(2)}) copy-start(bf16[480,480]{1,0:T(8,128)(2,1)} %param.20) | copy-start | bytes 1382404
  198.0 8.1 %collective-permute-start.3 = (bf16[1,256,480]{1,2,0:T(8,128)(2,1)S(1)}, bf16[1,256,480]{1,2,0:T(8,128)(2,1)S(1)}, u32[]{:S(2)}, u32[]{:S(2)}) collective-permute-start(bf16[1,256,480]{1,2,0:T(8,128)(2,1)S(1)} %convert_bitcast_fusion.2), channel_id=1, source_target_pairs={{0,1},{1,0},{2,3},{3,2},{4,5},{5,4},{6,7},{7,6},{8,9},{9,8},{10,11... | collective-permute-start | bytes 737288 | tf_op jit(solution)/shard_map/ppermute | solution.py:25
  207.7 44.6 %reduce-scatter.27.cloned.1.call-start = ((), (), s32[]{:S(2)}) async-start(), calls=%async_computation.24 | async-start | bytes 819200 | tf_op jit(solution)/shard_map/reduce_scatter | solution.py:273
  225.5 4.1 copy-start.23
  229.6 47.7 %reduce-scatter.25.cloned.1.call-start = ((), (), s32[]{:S(2)}) async-start(), calls=%async_computation.23 | async-start | bytes 819200 | tf_op jit(solution)/shard_map/reduce_scatter | solution.py:267
  230.8 5.1 copy-start.18
  230.8 5.1 copy-start.20
  234.6 1.3 copy-start.3
  237.5 56.1 %all-gather.3.cloned.1.call-start = ((), (), s32[]{:S(2)}) async-start(), calls=%async_computation.17 | async-start | bytes 1966080 | tf_op jit(solution)/shard_map/all_gather | solution.py:79
  238.1 93.4 %reduce-scatter.29.cloned.1.call-start = ((), (), s32[]{:S(2)}) async-start(), calls=%async_computation.25 | async-start | bytes 1474560 | tf_op jit(solution)/shard_map/reduce_scatter | solution.py:87
  277.3 14.6 %copy-start.28 = (bf16[480,160]{1,0:T(8,128)(2,1)S(1)}, bf16[480,160]{1,0:T(8,128)(2,1)}, u32[]{:S(2)}) copy-start(bf16[480,160]{1,0:T(8,128)(2,1)} %copy-done.27) | copy-start | bytes 460804
  277.3 14.6 %copy-start.30 = (bf16[480,160]{1,0:T(8,128)(2,1)S(1)}, bf16[480,160]{1,0:T(8,128)(2,1)}, u32[]{:S(2)}) copy-start(bf16[480,160]{1,0:T(8,128)(2,1)} %copy-done.29) | copy-start | bytes 460804
  277.3 14.6 %copy-start.38 = (bf16[480,480]{1,0:T(8,128)(2,1)S(1)}, bf16[480,480]{1,0:T(8,128)(2,1)}, u32[]{:S(2)}) copy-start(bf16[480,480]{1,0:T(8,128)(2,1)} %param.17) | copy-start | bytes 1382404
  291.0 0.9 copy-start.6
  293.5 69.3 %reduce-scatter.17.cloned.1.call-start = ((), (), s32[]{:S(2)}) async-start(), calls=%async_computation.18 | async-start | bytes 1474560 | tf_op jit(solution)/shard_map/reduce_scatter | solution.py:87
  306.9 362.5 %all-reduce.8.cloned.1.call-start = ((), (), s32[]{:S(2)}) async-start(), calls=%async_computation.26 | async-start | bytes 20971520 | tf_op jit(solution)/shard_map/psum | solution.py:308
  319.1 8.0 %copy-start.13 = (bf16[2,60,8,256]{3,2,0,1:T(8,128)(2,1)S(1)}, bf16[2,60,8,256]{3,2,0,1:T(8,128)(2,1)}, u32[]{:S(2)}) copy-start(bf16[2,60,8,256]{3,2,0,1:T(8,128)(2,1)} %copy-done.12) | copy-start | bytes 1474564
  325.7 1.4 copy-start.7
  329.6 0.7 copy-start.39
  329.6 1.9 copy-start.33
  329.6 3.2 copy-start.35
  329.6 33.3 %copy-start.5 = (f32[256,480]{0,1:T(8,128)S(1)}, f32[256,480]{0,1:T(8,128)}, u32[]{:S(2)}) copy-start(f32[256,480]{0,1:T(8,128)} %reduce-scatter.21.cloned.1.call-done) | copy-start | bytes 1474564
  329.7 33.2 %copy-start.11 = (bf16[256,480]{0,1:T(8,128)(2,1)S(1)}, bf16[256,480]{0,1:T(8,128)(2,1)}, u32[]{:S(2)}) copy-start(bf16[256,480]{0,1:T(8,128)(2,1)} %param.25) | copy-start | bytes 737284
  671.9 5.9 copy-start.26
  671.9 6.7 copy-start.25
  673.2 6.1 copy-start.21
Sparse Core Ops, SparseCore 0:
  24.8 10.5 reduce-scatter.10
  85.4 19.8 reduce-scatter.12
  121.6 10.4 reduce-scatter.18
  134.3 14.3 reduce-scatter.14
  153.7 12.6 all-gather.4
  171.4 20.8 reduce-scatter.20
  207.8 8.3 reduce-scatter.22
  229.7 22.5 reduce-scatter.26
  254.8 22.4 reduce-scatter.24
  279.2 9.3 all-gather.2
  293.7 19.6 reduce-scatter.28
  316.1 19.6 reduce-scatter.16
  341.9 327.5 all-reduce.7
